TPU v7x, 128 devices: a whole 4x4x4 slice. The times are simulated.
128 devices in a mesh: req: 8 (over x, y_hi), hid: 16 (over y_lo, z, core).
Axes of the slice: x: 4, y: 4 (y_hi: 2, y_lo: 2; y = y_hi * 2 + y_lo), z: 4, core: 2. Of those that a mesh axis runs over, the one named last changes fastest.
Arguments:
- input_activations: bfloat16 [8, 512, 4096], P('req'), may hold values from -6 to 6
- prompt_extents: int32 [8], P('req'), may hold values from 1 to 512, as said below
- continuing_flags: int32 [8], P('req'), may hold values from 0 to 1, as said below
- owning_index: int32 [8], P('req'), may hold values from 0 to 15
- partition_arrangement: int32 [128], replicated, may hold values from 0 to 127, each once
- training_accept_pieces: float32 [4096, 4096], P(('req', 'hid')), may hold values from -0.09375 to 0.09375
- training_lookup_pieces: float32 [4096, 4096], P(('req', 'hid')), may hold values from -0.09375 to 0.09375
- training_content_pieces: float32 [4096, 4096], P(('req', 'hid')), may hold values from -0.09375 to 0.09375
- normalizer_scales: bfloat16 [2, 4096], replicated, may hold values from 0.5 to 1.5
- prior_step_blends: bfloat16 [7, 4096], replicated, may hold values from 0.049804688 to 0.94921875
- forgetting_bias_vector: float32 [4096], P('hid'), may hold values from -7 to -3
- forgetting_left_lowrank: bfloat16 [4096, 128], replicated, may hold values from -0.09375 to 0.09375
- forgetting_right_lowrank: bfloat16 [128, 4096], P(None, 'hid'), may hold values from -0.5 to 0.5
- instant_emphasis: float32 [4096], P('hid'), may hold values from -3 to 3
- group_normalizer_scale: float32 [4096], P('hid'), may hold values from 0.5 to 1.5
- gating_projection: bfloat16 [4096, 4096], P(None, 'hid'), may hold values from -0.09375 to 0.09375
- mixing_exit_projection: bfloat16 [4096, 4096], P('hid'), may hold values from -0.09375 to 0.09375
- kept_summary_places: float32 [8, 16, 64, 64, 64], P('req', 'hid'), may hold values from -6 to 6
- previous_normed_entries: bfloat16 [8, 2, 4096], P('req'), may hold values from -6 to 6
- feedforward_entry_proj: bfloat16 [14336, 4096], P(('req', 'hid')), may hold values from -0.09375 to 0.09375
- feedforward_exit_proj: bfloat16 [14336, 4096], P(('req', 'hid')), may hold values from -0.046875 to 0.046875
- feedforward_accept_proj: bfloat16 [4096, 4096], P(None, 'hid'), may hold values from -0.09375 to 0.09375
Outputs:
- layer_out: bfloat16 [8, 512, 4096], P('req', None, 'hid')
- new_states: float32 [8, 64, 64, 64], P('req', 'hid')
- new_shift: bfloat16 [8, 2, 4096], P('req')
Inputs may be any that keep to these rules, and one draw needn't show every extreme that they name: `prompt_extents`: in every draw some request has length 512. `continuing_flags`: at least one request has 1 and at least one has 0. `owning_index`: read only where continuing_flags is 1. `partition_arrangement`: each of 0 to 127 appears once.
All inputs are finite; a program needn't handle non-finite values.
Results may differ from a plain program's by a relative error of at most 0.02.
Values may be sent and summed in bfloat16 or wider, within the bound.
A program may use at most 192 MiB of HBM per device.

v0:
```python
from functools import partial
import jax
import jax.numpy as jnp
from jax import lax
from jax.sharding import PartitionSpec as P

GROUP_DIMENSION = 64


def layer_norm(values, gain):
    center = values - jnp.mean(values, axis=-1, keepdims=True)
    spread = jnp.mean(center * center, axis=-1, keepdims=True)
    return center / jnp.sqrt(spread + 1e-05) * gain


def head_norm(outputs, gain_rows):
    center = outputs - jnp.mean(outputs, axis=-1, keepdims=True)
    spread = jnp.mean(center * center, axis=-1, keepdims=True)
    return center / jnp.sqrt(spread + 0.00064) * gain_rows


def shifted(values, first_row):
    return jnp.concatenate([first_row[None, :], values[:-1]], axis=0)


def segment_step(extra_diagonal_term, carried_summary, piece_sequence):
    acceptance_vectors, present_lookup_vectors, content_vectors, decays = piece_sequence
    inclusive = jnp.cumsum(decays, axis=0)
    exclusive = inclusive - decays
    closing = inclusive[-1]
    resulting_activations = jnp.einsum(
        "thi,hij->thj",
        acceptance_vectors * jnp.exp(exclusive),
        carried_summary,
        precision=lax.Precision.HIGHEST,
    )
    distance = exclusive[:, None] - inclusive[None, :]
    sizing = decays.shape[0]
    earlier = (jnp.arange(sizing)[:, None] > jnp.arange(sizing)[None, :]).astype(jnp.float32)
    factor = jnp.exp(jnp.minimum(distance, 0.0)) * earlier[:, :, None, None]
    scores = jnp.sum(
        acceptance_vectors[:, None] * factor * present_lookup_vectors[None, :], axis=-1
    )
    resulting_activations = resulting_activations + jnp.einsum(
        "tsh,shj->thj", scores, content_vectors, precision=lax.Precision.HIGHEST
    )
    resulting_activations = (
        resulting_activations
        + jnp.sum(
            acceptance_vectors * extra_diagonal_term * present_lookup_vectors,
            axis=-1,
            keepdims=True,
        )
        * content_vectors
    )
    weighted = present_lookup_vectors * jnp.exp(closing[None] - inclusive)
    carried_summary = jnp.exp(closing)[:, :, None] * carried_summary + jnp.einsum(
        "shi,shj->hij", weighted, content_vectors, precision=lax.Precision.HIGHEST
    )
    return (carried_summary, resulting_activations)


def local(
    input_activations,
    prompt_extents,
    continuing_flags,
    owning_index,
    partition_arrangement,
    training_accept_pieces,
    training_lookup_pieces,
    training_content_pieces,
    normalizer_scales,
    prior_step_blends,
    forgetting_bias_vector,
    forgetting_left_lowrank,
    forgetting_right_lowrank,
    instant_emphasis,
    group_normalizer_scale,
    gating_projection,
    mixing_exit_projection,
    kept_summary_places,
    previous_normed_entries,
    feedforward_entry_proj,
    feedforward_exit_proj,
    feedforward_accept_proj,
):
    token_rows = input_activations[0]
    seq_len, width = token_rows.shape
    local_width = mixing_exit_projection.shape[0]
    groups_on_device = local_width // GROUP_DIMENSION
    shards = partition_arrangement.shape[0]
    shard_rows = width // shards
    length = prompt_extents[0]
    resuming = continuing_flags[0]
    present = jnp.arange(seq_len) < length
    gain_rows = normalizer_scales.astype(jnp.float32)
    mix_rows = prior_step_blends.astype(jnp.float32)
    carried = previous_normed_entries[0].astype(jnp.float32)
    normed_in = layer_norm(token_rows.astype(jnp.float32), gain_rows[0])
    before = shifted(normed_in, jnp.where(resuming == 1, carried[0], 0.0))
    blended = (normed_in[None] + (before - normed_in)[None] * mix_rows[:5, None, :]).astype(
        jnp.bfloat16
    )
    permuted = jnp.take(
        blended[:3].reshape(3, seq_len, shards, shard_rows), partition_arrangement, axis=2
    ).reshape(3, seq_len, width)
    local_rows = jnp.stack(
        [training_accept_pieces, training_lookup_pieces, training_content_pieces]
    ).astype(jnp.bfloat16)
    collected = lax.all_gather(local_rows, "req", axis=1, tiled=True)
    swapped = lax.all_to_all(collected, "hid", split_axis=2, concat_axis=1, tiled=True)
    hid_count = lax.axis_size("hid")
    req_count = lax.axis_size("req")
    ordered = (
        swapped.reshape(3, hid_count, req_count, shard_rows, local_width)
        .transpose(0, 2, 1, 3, 4)
        .reshape(3, width, local_width)
    )
    projected = jnp.einsum("mtd,mdc->mtc", permuted, ordered, preferred_element_type=jnp.float32)
    low_rank = jnp.tanh(
        jnp.dot(blended[3], forgetting_left_lowrank, preferred_element_type=jnp.float32)
    ).astype(jnp.bfloat16)
    log_decay = -jnp.exp(
        forgetting_bias_vector
        + jnp.dot(low_rank, forgetting_right_lowrank, preferred_element_type=jnp.float32)
    )
    log_decay = jnp.where(present[:, None], log_decay, 0.0)
    gate = jax.nn.silu(jnp.dot(blended[4], gating_projection, preferred_element_type=jnp.float32))
    present_lookup_vectors = jnp.where(present[:, None], projected[1], 0.0)
    fetched = lax.all_to_all(
        kept_summary_places.astype(jnp.bfloat16), "hid", split_axis=2, concat_axis=1, tiled=True
    ).astype(kept_summary_places.dtype)
    chosen = lax.dynamic_index_in_dim(fetched[0], owning_index[0], 0, keepdims=False)
    carried_summary = jnp.where(resuming == 1, chosen, 0.0)
    block_len = min(64, seq_len)
    count_blocks = seq_len // block_len

    def by_blocks(values):
        return values.reshape(count_blocks, block_len, groups_on_device, GROUP_DIMENSION)

    sequences = (
        by_blocks(projected[0]),
        by_blocks(present_lookup_vectors),
        by_blocks(projected[2]),
        by_blocks(log_decay),
    )
    segment_cursor = partial(
        segment_step, instant_emphasis.reshape(groups_on_device, GROUP_DIMENSION)
    )
    carried_summary, outputs = lax.scan(segment_cursor, carried_summary, sequences)
    outputs = outputs.reshape(seq_len, groups_on_device, GROUP_DIMENSION)
    grouped = head_norm(
        outputs, group_normalizer_scale.reshape(groups_on_device, GROUP_DIMENSION)
    ).reshape(seq_len, local_width)
    gated = (grouped * gate).astype(jnp.bfloat16)
    head_terms = jnp.dot(gated, mixing_exit_projection, preferred_element_type=jnp.float32)
    attended = lax.psum(head_terms.astype(jnp.bfloat16), "hid").astype(jnp.float32)
    middle = (token_rows.astype(jnp.float32) + attended).astype(jnp.bfloat16)
    mid_share = lax.dynamic_slice_in_dim(
        middle, lax.axis_index("hid") * local_width, local_width, 1
    )
    chan_in = layer_norm(middle.astype(jnp.float32), gain_rows[1])
    chan_before = shifted(chan_in, jnp.where(resuming == 1, carried[1], 0.0))
    chan_mixed = (chan_in[None] + (chan_before - chan_in)[None] * mix_rows[5:, None, :]).astype(
        jnp.bfloat16
    )
    key_rows = lax.all_gather(feedforward_entry_proj, "req", axis=0, tiled=True)
    value_rows = lax.all_gather(feedforward_exit_proj, "req", axis=0, tiled=True)
    inner = lax.dot_general(
        chan_mixed[0], key_rows, (((1,), (1,)), ((), ())), preferred_element_type=jnp.float32
    )
    hidden = jnp.square(jnp.maximum(inner, 0.0)).astype(jnp.bfloat16)
    channel_terms = jnp.dot(hidden, value_rows, preferred_element_type=jnp.float32)
    mixed_out = lax.psum_scatter(
        channel_terms.astype(jnp.bfloat16), "hid", scatter_dimension=1, tiled=True
    ).astype(jnp.float32)
    gate_rows = jax.nn.sigmoid(
        jnp.dot(chan_mixed[1], feedforward_accept_proj, preferred_element_type=jnp.float32)
    )
    combined = mid_share.astype(jnp.float32) + gate_rows * mixed_out
    layer_out = jnp.where(present[:, None], combined, 0.0).astype(jnp.bfloat16)[None]
    last_index = length - 1
    shift_out = jnp.stack(
        [
            lax.dynamic_index_in_dim(normed_in, last_index, 0, keepdims=False),
            lax.dynamic_index_in_dim(chan_in, last_index, 0, keepdims=False),
        ]
    ).astype(jnp.bfloat16)[None]
    return (layer_out, carried_summary[None], shift_out)


def solution(mesh):
    placed = (
        P("req", None, None),
        P("req"),
        P("req"),
        P("req"),
        P(),
        P(("req", "hid"), None),
        P(("req", "hid"), None),
        P(("req", "hid"), None),
        P(),
        P(),
        P("hid"),
        P(),
        P(None, "hid"),
        P("hid"),
        P("hid"),
        P(None, "hid"),
        P("hid", None),
        P("req", "hid", None, None, None),
        P("req", None, None),
        P(("req", "hid"), None),
        P(("req", "hid"), None),
        P(None, "hid"),
    )
    return jax.shard_map(
        local,
        mesh=mesh,
        in_specs=placed,
        out_specs=(P("req", None, "hid"), P("req", "hid", None, None), P("req", None, None)),
        check_vma=False,
    )
```

profile of v0, /device:TPU:6, one launch (start us, length us, event | category | flops | bytes accessed | tf_op | source)
XLA Modules:
  0.0 817.3 jit_solution(10165721648546910749)
XLA Ops:
  7.2 1.2 convert_bitcast_fusion.3
  8.4 1.3 convert_bitcast_fusion.1
  10.7 1.8 fusion.60
  12.5 1.5 reshape.260
  14.0 6.4 all-to-all-start
  21.3 3.4 convert_reduce_fusion
  24.8 3.4 fusion.19
  28.3 1.8 fusion.20
  30.1 4.1 slice_bitcast_fusion.1
  34.2 1.7 copy-done.5
  36.6 67.1 %all-gather.4.cloned.1.call-done = bf16[3,256,4096]{2,1,0:T(8,128)(2,1)} async-done(((bf16[3,32,4096]{2,1,0:T(8,128)(2,1)}), bf16[3,256,4096]{2,1,0:T(8,128)(2,1)}) %all-gather.4.cloned.1.call-update) | async-done | bytes 6291472 | tf_op jit(solution)/shard_map/all_gather | solution.py:110
  103.7 13.1 %copy.123 = bf16[3,256,4096]{1,0,2:T(4,128)(2,1)} copy(bf16[3,256,4096]{2,1,0:T(8,128)(2,1)} %all-gather.4.cloned.1.call-done) | data formatting | bytes 12582912 | tf_op jit(solution)/shard_map/all_gather | solution.py:110
  116.8 4.8 all-to-all-start.1
  121.9 10.4 %fusion.27 = (f32[512,4096]{1,0:T(8,128)}, f32[512,4096]{1,0:T(8,128)}) fusion(bf16[1,512,4096]{2,1,0:T(8,128)(2,1)} %param.24, f32[4096]{0:T(1024)S(1)} %bitcast.201, f32[512]{0:T(512)S(1)} %add_sqrt_fusion.1, f32[512]{0:T(512)S(1)} %broadcast_multiply_fusion.1, f32[1,511,4096]{2,1,0:T(8,128)} %slice_bitcast_fusion.1, f32[1,1,4096]{2,1,0:T(1,128)S(1)} %get-tuple-element.126), kind=kLoop, calls=%fused_computation.55 | loop fusion | flops 12582912 | bytes 29380608 | tf_op jit(solution)/shard_map/add | solution.py:101
  132.3 9.0 %copy.120 = f32[512,4096]{0,1:T(8,128)} copy(f32[512,4096]{1,0:T(8,128)} %get-tuple-element.120) | data formatting | bytes 16777216 | tf_op jit(solution)/shard_map/add | solution.py:101
  141.3 9.0 %copy.121 = f32[512,4096]{0,1:T(8,128)} copy(f32[512,4096]{1,0:T(8,128)} %get-tuple-element.121) | data formatting | bytes 16777216 | tf_op jit(solution)/shard_map/mul | solution.py:101
  150.4 10.3 %add_convert_fusion = bf16[5,512,4096]{1,2,0:T(8,128)(2,1)S(1)} fusion(f32[5,4096]{1,0:T(8,128)S(1)} %slice.75, f32[512,4096]{0,1:T(8,128)} %copy.121, f32[512,4096]{0,1:T(8,128)} %copy.120), kind=kLoop, calls=%fused_computation.28 | loop fusion | flops 31457280 | bytes 37830656 | tf_op jit(solution)/shard_map/convert_element_type | solution.py:101
  160.7 6.5 slice.77
  167.2 4.2 copy-done.4
  171.4 12.8 %gather_fusion = bf16[128,3,512,32]{2,3,1,0:T(8,128)(2,1)} fusion(bf16[3,512,128,32]{1,3,2,0:T(8,128)(2,1)} %bitcast.190, s32[1024]{0:T(1024)S(1)} %pad_clamp_fusion), kind=kCustom, calls=%fused_computation | custom fusion | bytes 25166336 | tf_op jit(solution)/shard_map/jit(_take)/gather | solution.py:104
  184.2 10.7 %copy.122 = bf16[3,512,128,32]{1,3,2,0:T(8,128)(2,1)} copy(bf16[3,512,128,32]{1,3,0,2:T(8,128)(2,1)} %bitcast.191) | data formatting | bytes 25165824 | tf_op jit(solution)/shard_map/jit(_take)/gather | solution.py:104
  195.8 3.9 fusion.34
  199.8 1.5 reshape.245
  202.5 11.2 %bitcast_select_fusion = bf16[3,512,4096]{1,2,0:T(8,128)(2,1)} fusion(bf16[3,512,128,32]{1,3,2,0:T(8,128)(2,1)} %copy.122, pred[4096]{0:T(1024)(128)(4,1)S(1)} %broadcast_in_dim.95), kind=kLoop, calls=%fused_computation.30 | loop fusion | flops 6291456 | bytes 25169920 | tf_op jit(solution)/shard_map/jit(_take)/select_n | solution.py:104
  213.7 1.7 reshape.261
  216.2 27.1 %all-to-all-done.1 = bf16[3,256,4096]{1,0,2:T(4,128)(2,1)} async-done(((bf16[3,256,4096]{1,0,2:T(4,128)(2,1)}), bf16[3,256,4096]{1,0,2:T(4,128)(2,1)}, u32[]{:S(2)}, u32[]{:S(2)}) %all-to-all-start.1) | async-done | bytes 6291488 | tf_op jit(solution)/shard_map/all_to_all | solution.py:111
  243.3 6.9 copy.124
  250.2 9.1 %copy.125 = bf16[3,16,256,256]{3,2,1,0:T(8,128)(2,1)} copy(bf16[3,16,256,256]{2,3,1,0:T(8,128)(2,1)} %bitcast.193) | data formatting | bytes 12582912 | tf_op jit(solution)/shard_map/all_to_all | solution.py:111
  259.3 6.5 copy.126
  265.7 12.0 %fusion.61 = f32[3,512,256]{2,1,0:T(8,128)} fusion(bf16[3,512,4096]{1,2,0:T(8,128)(2,1)} %bitcast_select_fusion, bf16[3,4096,256]{2,1,0:T(8,128)(2,1)} %bitcast.196), kind=kOutput, calls=%fused_computation.119 | convolution fusion | flops 3221225472 | bytes 20447232 | tf_op jit(solution)/shard_map/mtd,mdc->mtc/dot_general | solution.py:119
  277.7 2.6 fusion.58
  280.2 1.5 squeeze.51
  281.7 2.5 reshape_squeeze.6
  284.2 2.4 reshape_squeeze.7
  286.6 1.5 broadcast_select_fusion
  288.1 79.8 %while.12 = (s32[]{:T(128)}, f32[4,64,64]{2,1,0:T(8,128)S(1)}, f32[8,64,4,64]{3,1,2,0:T(8,128)}, f32[8,64,4,64]{3,2,1,0:T(4,128)}, f32[8,64,4,64]{3,2,1,0:T(4,12...) while((s32[]{:T(128)}, f32[4,64,64]{2,1,0:T(8,128)S(1)}, ...), condition=%wide.region_6.7_spmd, body=%wide.region_2.6_spmd.sunk | while | flops 45260544 | bytes 2537577 | solution.py:150
  292.0 3.4 multiply_reduce_fusion.6
  302.0 3.4 multiply_reduce_fusion.6
  308.8 1.1 multiply_reduce_fusion.5
  311.9 3.4 multiply_reduce_fusion.6
  318.7 1.1 multiply_reduce_fusion.5
  321.9 3.4 multiply_reduce_fusion.6
  328.6 1.1 multiply_reduce_fusion.5
  331.8 3.4 multiply_reduce_fusion.6
  338.6 1.1 multiply_reduce_fusion.5
  341.8 3.4 multiply_reduce_fusion.6
  351.7 3.4 multiply_reduce_fusion.6
  361.7 3.4 multiply_reduce_fusion.6
  367.9 2.0 copy.130
  369.8 1.6 reduce_sum.74
  371.5 1.4 reshape.249
  372.9 1.9 multiply_reduce_fusion.2
  376.3 9.6 %convolution_convert_fusion.1 = bf16[512,4096]{1,0:T(8,128)(2,1)} fusion(bf16[256,4096]{1,0:T(8,128)(2,1)S(1)} %copy-done, bf16[4096,256]{1,0:T(8,128)(2,1)} %param.39, bf16[5,512,4096]{1,2,0:T(8,128)(2,1)} %copy-done.4, f32[512,256]{1,0:T(8,128)S(1)} %copy.135, f32[512,256]{1,0:T(8,128)} %reshape.249, f32[512,256]{1,0:T(8,128)} %copy.132, ...), kind=kOutput, calls=%fused_computation.54 | convolution fusion | flops 2150760448 | bytes 14156800 | tf_op jit(solution)/shard_map/dot_general | solution.py:156
  387.2 135.4 %all-reduce.2.cloned.1.call-done = bf16[512,4096]{1,0:T(8,128)(2,1)} async-done(((bf16[512,4096]{1,0:T(8,128)(2,1)}), bf16[512,4096]{1,0:T(8,128)(2,1)}) %all-reduce.2.cloned.1.call-update) | async-done | bytes 4194320 | tf_op jit(solution)/shard_map/psum | solution.py:157
  522.7 5.2 convert_reduce_fusion.1
  527.9 1.2 fusion.21
  529.1 2.1 fusion.22
  531.2 3.5 maximum_subtract_fusion.1
  534.7 4.8 add_convert_fusion.1
  539.5 83.5 %all-gather.6.cloned.1.call-done = bf16[896,4096]{1,0:T(8,128)(2,1)} async-done(((bf16[112,4096]{1,0:T(8,128)(2,1)}), bf16[896,4096]{1,0:T(8,128)(2,1)}) %all-gather.6.cloned.1.call-update) | async-done | bytes 7340048 | tf_op jit(solution)/shard_map/all_gather | solution.py:167
  623.0 99.4 %all-gather.8.cloned.1.call-done = bf16[896,4096]{1,0:T(8,128)(2,1)} async-done(((bf16[112,4096]{1,0:T(8,128)(2,1)}), bf16[896,4096]{1,0:T(8,128)(2,1)}) %all-gather.8.cloned.1.call-update) | async-done | bytes 7340048 | tf_op jit(solution)/shard_map/all_gather | solution.py:168
  722.4 16.2 %convolution_convert_fusion = bf16[512,4096]{1,0:T(8,128)(2,1)} fusion(bf16[896,4096]{1,0:T(8,128)(2,1)} %all-gather.8.cloned.1.call-done, bf16[896,4096]{1,0:T(8,128)(2,1)} %all-gather.6.cloned.1.call-done, bf16[2,512,4096]{2,1,0:T(8,128)(2,1)} %add_convert_fusion.1), kind=kOutput, calls=%fused_computation.53 | convolution fusion | flops 7519666176 | bytes 23068672 | tf_op jit(solution)/shard_map/dot_general | solution.py:173
  741.1 64.5 %reduce-scatter.2.cloned.1.call-done = bf16[512,256]{1,0:T(8,128)(2,1)} async-done(((bf16[512,4096]{1,0:T(8,128)(2,1)}), bf16[512,256]{1,0:T(8,128)(2,1)}) %reduce-scatter.2.cloned.1.call-update) | async-done | bytes 262160 | tf_op jit(solution)/shard_map/reduce_scatter | solution.py:174
  805.6 4.9 fusion.45
  (186 shorter events, 56.6 us)
Async XLA Ops:
  7.2 369.1 %copy-start = (bf16[256,4096]{1,0:T(8,128)(2,1)S(1)}, bf16[256,4096]{1,0:T(8,128)(2,1)}, u32[]{:S(2)}) copy-start(bf16[256,4096]{1,0:T(8,128)(2,1)} %param.40) | copy-start | bytes 6291460
  7.2 14.1 %copy-start.11 = (bf16[1,2,4096]{2,1,0:T(2,128)(2,1)S(1)}, bf16[1,2,4096]{2,1,0:T(2,128)(2,1)}, u32[]{:S(2)}) copy-start(bf16[1,2,4096]{2,1,0:T(2,128)(2,1)} %param.42) | copy-start | bytes 49156
  7.2 96.5 %all-gather.4.cloned.1.call-start = ((), (), s32[]{:S(2)}) async-start(), calls=%async_computation.3 | async-start | bytes 7077888 | tf_op jit(solution)/shard_map/all_gather | solution.py:110
  9.7 18.5 %copy-start.9 = (bf16[2,4096]{1,0:T(2,128)(2,1)S(1)}, bf16[2,4096]{1,0:T(2,128)(2,1)}, u32[]{:S(2)}) copy-start(bf16[2,4096]{1,0:T(2,128)(2,1)} %param.32) | copy-start | bytes 49156
  14.0 102.8 %all-to-all-start = ((bf16[16,2,8192]{2,1,0:T(2,128)(2,1)}), bf16[16,2,8192]{2,1,0:T(2,128)(2,1)S(1)}, u32[]{:S(2)}, u32[]{:S(2)}) async-start(bf16[16,2,8192]{2,1,0:T(2,128)(2,1)} %reshape.260), calls=%async_computation | async-start | bytes 1048576 | tf_op jit(solution)/shard_map/all_to_all | solution.py:130
  20.5 7.8 copy-start.1
  30.1 5.8 copy-start.5
  116.8 126.4 %all-to-all-start.1 = ((bf16[3,256,4096]{1,0,2:T(4,128)(2,1)}), bf16[3,256,4096]{1,0,2:T(4,128)(2,1)}, u32[]{:S(2)}, u32[]{:S(2)}) async-start(bf16[3,256,4096]{1,0,2:T(4,128)(2,1)} %copy.123), calls=%async_computation.1 | async-start | bytes 16777216 | tf_op jit(solution)/shard_map/all_to_all | solution.py:111
  121.6 401.1 %all-reduce.2.cloned.1.call-start = ((), (), s32[]{:S(2)}) async-start(), calls=%async_computation.4 | async-start | bytes 8388608 | tf_op jit(solution)/shard_map/psum | solution.py:157
  141.3 9.0 %copy-start.7 = (bf16[7,4096]{1,0:T(8,128)(2,1)S(1)}, bf16[7,4096]{1,0:T(8,128)(2,1)}, u32[]{:S(2)}) copy-start(bf16[7,4096]{1,0:T(8,128)(2,1)} %param.33) | copy-start | bytes 172036
  160.7 10.7 %copy-start.4 = (bf16[5,512,4096]{1,2,0:T(8,128)(2,1)}, bf16[5,512,4096]{1,2,0:T(8,128)(2,1)S(1)}, u32[]{:S(2)}) copy-start(bf16[5,512,4096]{1,2,0:T(8,128)(2,1)S(1)} %add_convert_fusion) | copy-start | bytes 62914564
  160.7 10.7 %copy-start.16 = (s32[128]{0:T(128)S(1)}, s32[128]{0:T(128)}, u32[]{:S(2)}) copy-start(s32[128]{0:T(128)} %param.28) | copy-start | bytes 1540
  184.2 11.6 %copy-start.13 = (bf16[128,256]{1,0:T(8,128)(2,1)S(1)}, bf16[128,256]{1,0:T(8,128)(2,1)}, u32[]{:S(2)}) copy-start(bf16[128,256]{1,0:T(8,128)(2,1)} %param.36) | copy-start | bytes 196612
  184.2 11.6 %copy-start.14 = (f32[256]{0:T(256)S(1)}, f32[256]{0:T(256)}, u32[]{:S(2)}) copy-start(f32[256]{0:T(256)} %param.34) | copy-start | bytes 3076
  195.8 17.8 %copy-start.17 = (pred[512]{0:T(512)(128)(4,1)}, pred[512]{0:T(512)(128)(4,1)S(1)}, u32[]{:S(2)}) copy-start(pred[512]{0:T(512)(128)(4,1)S(1)} %iota_compare_fusion.1) | copy-start | bytes 1540
  265.7 20.9 %copy-start.12 = (pred[8,64]{1,0:T(8,128)(4,1)S(1)}, pred[8,64]{1,0:T(8,128)(4,1)}, u32[]{:S(2)}) copy-start(pred[8,64]{1,0:T(8,128)(4,1)} %add_compare_fusion) | copy-start | bytes 1540
  367.9 18.0 %copy-start.6 = (f32[4,64,64]{2,1,0:T(8,128)}, f32[4,64,64]{2,1,0:T(8,128)S(1)}, u32[]{:S(2)}) copy-start(f32[4,64,64]{2,1,0:T(8,128)S(1)} %get-tuple-element.47) | copy-start | bytes 196612
  367.9 8.4 %copy-start.15 = (f32[256]{0:T(256)S(1)}, f32[256]{0:T(256)}, u32[]{:S(2)}) copy-start(f32[256]{0:T(256)} %param.38) | copy-start | bytes 3076
  376.3 11.0 %copy-start.8 = (bf16[7,4096]{1,0:T(8,128)(2,1)S(1)}, bf16[7,4096]{1,0:T(8,128)(2,1)}, u32[]{:S(2)}) copy-start(bf16[7,4096]{1,0:T(8,128)(2,1)} %param.33) | copy-start | bytes 172036
  385.8 237.2 %all-gather.6.cloned.1.call-start = ((), (), s32[]{:S(2)}) async-start(), calls=%async_computation.5 | async-start | bytes 8257536 | tf_op jit(solution)/shard_map/all_gather | solution.py:167
  386.6 335.8 %all-gather.8.cloned.1.call-start = ((), (), s32[]{:S(2)}) async-start(), calls=%async_computation.6 | async-start | bytes 8257536 | tf_op jit(solution)/shard_map/all_gather | solution.py:168
  387.2 418.5 %reduce-scatter.2.cloned.1.call-start = ((), (), s32[]{:S(2)}) async-start(), calls=%async_computation.7 | async-start | bytes 4456448 | tf_op jit(solution)/shard_map/reduce_scatter | solution.py:174
  527.8 3.4 copy-start.3
  527.8 3.4 copy-start.10
  531.2 3.5 copy-start.2
  539.5 266.1 %copy-start.18 = (pred[512]{0:T(512)(128)(4,1)S(1)}, pred[512]{0:T(512)(128)(4,1)}, u32[]{:S(2)}) copy-start(pred[512]{0:T(512)(128)(4,1)} %copy-done.17) | copy-start | bytes 1540
Sparse Core Ops, SparseCore 0:
  10.8 92.8 all-gather.3
  386.0 136.6 all-reduce.1
  525.0 97.9 all-gather.5
  625.2 97.1 all-gather.7
  738.7 66.8 reduce-scatter.1
where the time goes:
time: 824 us; the launch traced here: 817 us
  waiting for transfers between devices  478 us (58%)
  local copies, waits for them, and re-layouts  128 us (16%)
  other arithmetic  122 us (15%)
  matrix products  59.3 us (7%)
  between operations  16.6 us (2%)
  starting transfers between devices  11.7 us (1%)
    psum x1, waiting for transfers between devices, local(): lax.psum(head_terms.astype(jnp.bfloat16), 'hid').astype(jnp.float32)  135 us
    all_gather x1, waiting for transfers between devices, local(): lax.all_gather(feedforward_exit_proj, 'req', axis=0, tiled=True)  99.4 us
    all_gather x1, waiting for transfers between devices, local(): key_rows = lax.all_gather(feedforward_entry_proj, 'req', axis=0, tiled=True)  83.5 us
    all_gather x1, waiting for transfers between devices, local(): collected = lax.all_gather(local_rows, 'req', axis=1, tiled=True)  67.1 us
    reduce_scatter x1, waiting for transfers between devices, local(): lax.psum_scatter(channel_terms.astype(jnp.bfloat16), 'hid', scatter_dimen...  64.5 us
    all_to_all x1, waiting for transfers between devices, local(): lax.all_to_all(collected, 'hid', split_axis=2, concat_axis=1, tiled=True)  27.1 us
    reduce_sum x8, other arithmetic, segment_step(): jnp.sum(acceptance_vectors[:, None] * factor * present_lookup_vectors[Non...  27 us
    gather x2, local copies, waits for them, and re-layouts, local(): jnp.take(blended[:3].reshape(3, seq_len, shards, shard_rows), partition_a...  23.5 us
  transfers between devices with their start and end apart: 7, of which 6 were waited for; matrix products, arithmetic and copies ran while one was open for 17% of the time, Pallas kernels for 0%

commit v1 on v0

--- a/solution.py
+++ b/solution.py
@@ -5,6 +5,14 @@
 from jax.sharding import PartitionSpec as P
 
 GROUP_DIMENSION = 64
+
+
+def _end_members_all(my_tile):
+    far_arr = lax.axis_size("req")
+    y2 = jnp.stack(far_arr * [my_tile], axis=0)
+    oldest = lax.all_to_all(y2, split_axis=0, concat_axis=0, axis_name="req")
+    b_now = jnp.concatenate(oldest, axis=1)
+    return b_now
 
 
 def layer_norm(values, gain):
@@ -107,7 +115,7 @@
     local_rows = jnp.stack(
         [training_accept_pieces, training_lookup_pieces, training_content_pieces]
     ).astype(jnp.bfloat16)
-    collected = lax.all_gather(local_rows, "req", axis=1, tiled=True)
+    collected = _end_members_all(local_rows)
     swapped = lax.all_to_all(collected, "hid", split_axis=2, concat_axis=1, tiled=True)
     hid_count = lax.axis_size("hid")
     req_count = lax.axis_size("req")

time: 824 us -> 747 us (0.907)
  waiting for transfers between devices: 478 us -> 381 us
  local copies, waits for them, and re-layouts: 128 us -> 139 us
    all_gather x1, waiting for transfers between devices: 99.4 us -> 0.01 us  [local(): lax.all_gather(feedforward_exit_proj, 'req', axis=0, tiled=True)]
    all_gather x1, waiting for transfers between devices: 83.5 us -> 0.01 us  [local(): key_rows = lax.all_gather(feedforward_entry_proj, 'req', axis=0, tiled=True)]
    psum x1, waiting for transfers between devices: 135 us -> 218 us  [local(): lax.psum(head_terms.astype(jnp.bfloat16), 'hid').astype(jnp.float32)]
    all_gather x1 -> x0, waiting for transfers between devices: 67.1 us -> none  [local(): collected = lax.all_gather(local_rows, 'req', axis=1, tiled=True)]
    all_to_all x0 -> x1, waiting for transfers between devices: none -> 66.8 us  [_end_members_all(): oldest = lax.all_to_all(y2, split_axis=0, concat_axis=0, axis_name='req')]
    all_gather x1 -> x0, local copies, waits for them, and re-layouts: 13.1 us -> none  [local(): collected = lax.all_gather(local_rows, 'req', axis=1, tiled=True)]
    reshape x0 -> x1, local copies, waits for them, and re-layouts: none -> 13.1 us  [_end_members_all(): b_now = jnp.concatenate(oldest, axis=1)]
  transfers between devices with their start and end apart: 7 -> 7, of which waited for: 6 -> 4; matrix products, arithmetic and copies ran while one was open for 17% -> 19% of each run, Pallas kernels for 0% -> 0%
where the time goes in v1:
time: 747 us; the launch traced here: 738 us
  waiting for transfers between devices  381 us (51%)
  local copies, waits for them, and re-layouts  139 us (19%)
  other arithmetic  121 us (16%)
  matrix products  59.2 us (8%)
  starting transfers between devices  19.2 us (3%)
  between operations  18.1 us (2%)
    psum x1, waiting for transfers between devices, local(): lax.psum(head_terms.astype(jnp.bfloat16), 'hid').astype(jnp.float32)  218 us
    all_to_all x1, waiting for transfers between devices, _end_members_all(): oldest = lax.all_to_all(y2, split_axis=0, concat_axis=0, axis_name='req')  66.8 us
    reduce_scatter x1, waiting for transfers between devices, local(): lax.psum_scatter(channel_terms.astype(jnp.bfloat16), 'hid', scatter_dimen...  66.8 us
    all_to_all x1, waiting for transfers between devices, local(): lax.all_to_all(collected, 'hid', split_axis=2, concat_axis=1, tiled=True)  28.4 us
    reduce_sum x8, other arithmetic, segment_step(): jnp.sum(acceptance_vectors[:, None] * factor * present_lookup_vectors[Non...  27 us
    gather x2, local copies, waits for them, and re-layouts, local(): jnp.take(blended[:3].reshape(3, seq_len, shards, shard_rows), partition_a...  23.5 us
    dot_general x1, matrix products, local(): jnp.dot(hidden, value_rows, preferred_element_type=jnp.float32)  16.2 us
    all_to_all x2, local copies, waits for them, and re-layouts, local(): lax.all_to_all(collected, 'hid', split_axis=2, concat_axis=1, tiled=True)  15.9 us
  transfers between devices with their start and end apart: 7, of which 4 were waited for; matrix products, arithmetic and copies ran while one was open for 19% of the time, Pallas kernels for 0%

profile of v1, /device:TPU:6, one launch (start us, length us, event | category | flops | bytes accessed | tf_op | source)
XLA Modules:
  0.0 738.4 jit_solution(16997256432424297213)
XLA Ops:
  8.0 1.2 convert_bitcast_fusion.3
  9.2 1.3 convert_bitcast_fusion.1
  10.6 3.3 stack.36
  13.9 7.4 %all-to-all-start.1 = ((bf16[8,3,32,4096]{3,2,1,0:T(8,128)(2,1)}), bf16[8,3,32,4096]{3,2,1,0:T(8,128)(2,1)}, u32[]{:S(2)}, u32[]{:S(2)}) async-start(bf16[8,3,32,4096]{3,2,1,0:T(8,128)(2,1)} %stack.36), calls=%async_computation.1 | async-start | bytes 12582912 | tf_op jit(solution)/shard_map/all_to_all | solution.py:13
  22.1 1.8 fusion.60
  23.9 1.5 reshape.284
  25.4 3.0 convert_reduce_fusion
  28.3 3.4 fusion.19
  31.8 1.8 fusion.20
  33.7 3.3 copy-done.5
  37.0 3.8 slice_bitcast_fusion.1
  40.7 66.8 %all-to-all-done.1 = bf16[8,3,32,4096]{3,2,1,0:T(8,128)(2,1)} async-done(((bf16[8,3,32,4096]{3,2,1,0:T(8,128)(2,1)}), bf16[8,3,32,4096]{3,2,1,0:T(8,128)(2,1)}, u32[]{:S(2)}, u32[]{:S(2)}) %all-to-all-start.1) | async-done | bytes 6291488 | tf_op jit(solution)/shard_map/all_to_all | solution.py:13
  107.6 5.5 all-to-all-start
  113.7 6.1 copy.127
  119.9 13.1 %copy.128 = bf16[3,256,4096]{1,0,2:T(4,128)(2,1)} copy(bf16[3,256,4096]{2,1,0:T(8,128)(2,1)} %bitcast.196) | data formatting | bytes 12582912 | tf_op jit(solution)/shard_map/reshape | solution.py:14
  133.0 5.8 all-to-all-start.2
  139.1 10.4 %fusion.27 = (f32[512,4096]{1,0:T(8,128)}, f32[512,4096]{1,0:T(8,128)}) fusion(bf16[1,512,4096]{2,1,0:T(8,128)(2,1)} %param.24, f32[4096]{0:T(1024)S(1)} %bitcast.205, f32[512]{0:T(512)S(1)} %add_sqrt_fusion.1, f32[512]{0:T(512)S(1)} %broadcast_multiply_fusion.1, f32[1,511,4096]{2,1,0:T(8,128)} %slice_bitcast_fusion.1, f32[1,1,4096]{2,1,0:T(1,128)S(1)} %get-tuple-element.126), kind=kLoop, calls=%fused_computation.55 | loop fusion | flops 12582912 | bytes 29380608 | tf_op jit(solution)/shard_map/add | solution.py:109
  149.5 9.0 %copy.124 = f32[512,4096]{0,1:T(8,128)} copy(f32[512,4096]{1,0:T(8,128)} %get-tuple-element.120) | data formatting | bytes 16777216 | tf_op jit(solution)/shard_map/add | solution.py:109
  158.5 9.0 %copy.125 = f32[512,4096]{0,1:T(8,128)} copy(f32[512,4096]{1,0:T(8,128)} %get-tuple-element.121) | data formatting | bytes 16777216 | tf_op jit(solution)/shard_map/mul | solution.py:109
  167.5 10.3 %add_convert_fusion = bf16[5,512,4096]{1,2,0:T(8,128)(2,1)S(1)} fusion(f32[5,4096]{1,0:T(8,128)S(1)} %slice.75, f32[512,4096]{0,1:T(8,128)} %copy.125, f32[512,4096]{0,1:T(8,128)} %copy.124), kind=kLoop, calls=%fused_computation.28 | loop fusion | flops 31457280 | bytes 37830656 | tf_op jit(solution)/shard_map/convert_element_type | solution.py:109
  177.9 6.5 slice.77
  184.4 4.2 copy-done.4
  188.6 12.8 %gather_fusion = bf16[128,3,512,32]{2,3,1,0:T(8,128)(2,1)} fusion(bf16[3,512,128,32]{1,3,2,0:T(8,128)(2,1)} %bitcast.193, s32[1024]{0:T(1024)S(1)} %pad_clamp_fusion), kind=kCustom, calls=%fused_computation | custom fusion | bytes 25166336 | tf_op jit(solution)/shard_map/jit(_take)/gather | solution.py:112
  201.4 10.7 %copy.126 = bf16[3,512,128,32]{1,3,2,0:T(8,128)(2,1)} copy(bf16[3,512,128,32]{1,3,0,2:T(8,128)(2,1)} %bitcast.194) | data formatting | bytes 25165824 | tf_op jit(solution)/shard_map/jit(_take)/gather | solution.py:112
  213.0 3.9 fusion.34
  217.0 1.5 reshape.267
  219.6 11.2 %bitcast_select_fusion = bf16[3,512,4096]{1,2,0:T(8,128)(2,1)} fusion(bf16[3,512,128,32]{1,3,2,0:T(8,128)(2,1)} %copy.126, pred[4096]{0:T(1024)(128)(4,1)S(1)} %broadcast_in_dim.95), kind=kLoop, calls=%fused_computation.30 | loop fusion | flops 6291456 | bytes 25169920 | tf_op jit(solution)/shard_map/jit(_take)/select_n | solution.py:112
  230.8 1.7 reshape.285
  233.3 28.4 %all-to-all-done.2 = bf16[3,256,4096]{1,0,2:T(4,128)(2,1)} async-done(((bf16[3,256,4096]{1,0,2:T(4,128)(2,1)}), bf16[3,256,4096]{1,0,2:T(4,128)(2,1)}, u32[]{:S(2)}, u32[]{:S(2)}) %all-to-all-start.2) | async-done | bytes 6291488 | tf_op jit(solution)/shard_map/all_to_all | solution.py:119
  261.7 6.9 copy.129
  268.6 9.1 %copy.130 = bf16[3,16,256,256]{3,2,1,0:T(8,128)(2,1)} copy(bf16[3,16,256,256]{2,3,1,0:T(8,128)(2,1)} %bitcast.197) | data formatting | bytes 12582912 | tf_op jit(solution)/shard_map/all_to_all | solution.py:119
  277.7 6.5 copy.131
  284.1 12.0 %fusion.61 = f32[3,512,256]{2,1,0:T(8,128)} fusion(bf16[3,512,4096]{1,2,0:T(8,128)(2,1)} %bitcast_select_fusion, bf16[3,4096,256]{2,1,0:T(8,128)(2,1)} %bitcast.200), kind=kOutput, calls=%fused_computation.119 | convolution fusion | flops 3221225472 | bytes 20447232 | tf_op jit(solution)/shard_map/mtd,mdc->mtc/dot_general | solution.py:127
  296.1 2.5 fusion.58
  298.6 1.5 squeeze.51
  300.1 2.5 reshape_squeeze.6
  302.6 2.4 reshape_squeeze.7
  305.0 1.5 broadcast_select_fusion
  306.5 79.7 %while.12 = (s32[]{:T(128)}, f32[4,64,64]{2,1,0:T(8,128)S(1)}, f32[8,64,4,64]{3,1,2,0:T(8,128)}, f32[8,64,4,64]{3,2,1,0:T(4,128)}, f32[8,64,4,64]{3,2,1,0:T(4,12...) while((s32[]{:T(128)}, f32[4,64,64]{2,1,0:T(8,128)S(1)}, ...), condition=%wide.region_6.7_spmd, body=%wide.region_2.6_spmd.sunk | while | flops 45260544 | bytes 2537577 | solution.py:158
  307.2 1.1 multiply_reduce_fusion.5
  310.4 3.4 multiply_reduce_fusion.6
  320.4 3.4 multiply_reduce_fusion.6
  327.1 1.1 multiply_reduce_fusion.5
  330.3 3.4 multiply_reduce_fusion.6
  340.3 3.4 multiply_reduce_fusion.6
  347.0 1.1 multiply_reduce_fusion.5
  350.2 3.4 multiply_reduce_fusion.6
  360.1 3.4 multiply_reduce_fusion.6
  370.1 3.4 multiply_reduce_fusion.6
  380.1 3.4 multiply_reduce_fusion.6
  386.2 2.0 copy.135
  388.2 1.6 reduce_sum.74
  389.9 1.4 reshape.273
  391.3 1.9 multiply_reduce_fusion.2
  394.6 9.6 %convolution_convert_fusion.1 = bf16[512,4096]{1,0:T(8,128)(2,1)} fusion(bf16[256,4096]{1,0:T(8,128)(2,1)S(1)} %copy-done, bf16[4096,256]{1,0:T(8,128)(2,1)} %param.39, bf16[5,512,4096]{1,2,0:T(8,128)(2,1)} %copy-done.4, f32[512,256]{1,0:T(8,128)S(1)} %copy.140, f32[512,256]{1,0:T(8,128)} %reshape.273, f32[512,256]{1,0:T(8,128)} %copy.137, ...), kind=kOutput, calls=%fused_computation.54 | convolution fusion | flops 2150760448 | bytes 14156800 | tf_op jit(solution)/shard_map/dot_general | solution.py:164
  405.4 218.0 %all-reduce.2.cloned.1.call-done = bf16[512,4096]{1,0:T(8,128)(2,1)} async-done(((bf16[512,4096]{1,0:T(8,128)(2,1)}), bf16[512,4096]{1,0:T(8,128)(2,1)}) %all-reduce.2.cloned.1.call-update) | async-done | bytes 4194320 | tf_op jit(solution)/shard_map/psum | solution.py:165
  623.5 5.2 convert_reduce_fusion.1
  628.7 1.2 fusion.21
  629.9 2.1 fusion.22
  632.1 3.5 maximum_subtract_fusion.1
  635.5 4.8 add_convert_fusion.1
  640.4 16.2 %convolution_convert_fusion = bf16[512,4096]{1,0:T(8,128)(2,1)} fusion(bf16[896,4096]{1,0:T(8,128)(2,1)} %all-gather.5.cloned.1.call-done, bf16[896,4096]{1,0:T(8,128)(2,1)} %all-gather.3.cloned.1.call-done, bf16[2,512,4096]{2,1,0:T(8,128)(2,1)} %add_convert_fusion.1), kind=kOutput, calls=%fused_computation.53 | convolution fusion | flops 7519666176 | bytes 23068672 | tf_op jit(solution)/shard_map/dot_general | solution.py:181
  659.1 66.8 %reduce-scatter.2.cloned.1.call-done = bf16[512,256]{1,0:T(8,128)(2,1)} async-done(((bf16[512,4096]{1,0:T(8,128)(2,1)}), bf16[512,256]{1,0:T(8,128)(2,1)}) %reduce-scatter.2.cloned.1.call-update) | async-done | bytes 262160 | tf_op jit(solution)/shard_map/reduce_scatter | solution.py:182
  725.9 4.9 fusion.45
  (187 shorter events, 56.6 us)
Async XLA Ops:
  8.0 386.6 %copy-start = (bf16[256,4096]{1,0:T(8,128)(2,1)S(1)}, bf16[256,4096]{1,0:T(8,128)(2,1)}, u32[]{:S(2)}) copy-start(bf16[256,4096]{1,0:T(8,128)(2,1)} %param.40) | copy-start | bytes 6291460
  10.6 11.4 %copy-start.11 = (bf16[1,2,4096]{2,1,0:T(2,128)(2,1)S(1)}, bf16[1,2,4096]{2,1,0:T(2,128)(2,1)}, u32[]{:S(2)}) copy-start(bf16[1,2,4096]{2,1,0:T(2,128)(2,1)} %param.42) | copy-start | bytes 49156
  13.9 93.6 %all-to-all-start.1 = ((bf16[8,3,32,4096]{3,2,1,0:T(8,128)(2,1)}), bf16[8,3,32,4096]{3,2,1,0:T(8,128)(2,1)}, u32[]{:S(2)}, u32[]{:S(2)}) async-start(bf16[8,3,32,4096]{3,2,1,0:T(8,128)(2,1)} %stack.36), calls=%async_computation.1 | async-start | bytes 12582912 | tf_op jit(solution)/shard_map/all_to_all | solution.py:13
  21.4 10.4 %copy-start.9 = (bf16[2,4096]{1,0:T(2,128)(2,1)S(1)}, bf16[2,4096]{1,0:T(2,128)(2,1)}, u32[]{:S(2)}) copy-start(bf16[2,4096]{1,0:T(2,128)(2,1)} %param.32) | copy-start | bytes 49156
  25.4 6.4 copy-start.1
  33.7 3.3 copy-start.5
  107.6 25.4 %all-to-all-start = ((bf16[16,2,8192]{2,1,0:T(2,128)(2,1)}), bf16[16,2,8192]{2,1,0:T(2,128)(2,1)S(1)}, u32[]{:S(2)}, u32[]{:S(2)}) async-start(bf16[16,2,8192]{2,1,0:T(2,128)(2,1)} %reshape.284), calls=%async_computation | async-start | bytes 1048576 | tf_op jit(solution)/shard_map/all_to_all | solution.py:138
  133.0 128.7 %all-to-all-start.2 = ((bf16[3,256,4096]{1,0,2:T(4,128)(2,1)}), bf16[3,256,4096]{1,0,2:T(4,128)(2,1)}, u32[]{:S(2)}, u32[]{:S(2)}) async-start(bf16[3,256,4096]{1,0,2:T(4,128)(2,1)} %copy.128), calls=%async_computation.2 | async-start | bytes 16777216 | tf_op jit(solution)/shard_map/all_to_all | solution.py:119
  138.8 484.7 %all-reduce.2.cloned.1.call-start = ((), (), s32[]{:S(2)}) async-start(), calls=%async_computation.4 | async-start | bytes 8388608 | tf_op jit(solution)/shard_map/psum | solution.py:165
  158.5 9.0 %copy-start.7 = (bf16[7,4096]{1,0:T(8,128)(2,1)S(1)}, bf16[7,4096]{1,0:T(8,128)(2,1)}, u32[]{:S(2)}) copy-start(bf16[7,4096]{1,0:T(8,128)(2,1)} %param.33) | copy-start | bytes 172036
  177.8 10.7 %copy-start.4 = (bf16[5,512,4096]{1,2,0:T(8,128)(2,1)}, bf16[5,512,4096]{1,2,0:T(8,128)(2,1)S(1)}, u32[]{:S(2)}) copy-start(bf16[5,512,4096]{1,2,0:T(8,128)(2,1)S(1)} %add_convert_fusion) | copy-start | bytes 62914564
  177.9 10.7 %copy-start.16 = (s32[128]{0:T(128)S(1)}, s32[128]{0:T(128)}, u32[]{:S(2)}) copy-start(s32[128]{0:T(128)} %param.28) | copy-start | bytes 1540
  201.4 11.6 %copy-start.13 = (bf16[128,256]{1,0:T(8,128)(2,1)S(1)}, bf16[128,256]{1,0:T(8,128)(2,1)}, u32[]{:S(2)}) copy-start(bf16[128,256]{1,0:T(8,128)(2,1)} %param.36) | copy-start | bytes 196612
  201.4 11.6 %copy-start.14 = (f32[256]{0:T(256)S(1)}, f32[256]{0:T(256)}, u32[]{:S(2)}) copy-start(f32[256]{0:T(256)} %param.34) | copy-start | bytes 3076
  213.0 17.8 %copy-start.17 = (pred[512]{0:T(512)(128)(4,1)}, pred[512]{0:T(512)(128)(4,1)S(1)}, u32[]{:S(2)}) copy-start(pred[512]{0:T(512)(128)(4,1)S(1)} %iota_compare_fusion.1) | copy-start | bytes 1540
  284.1 20.9 %copy-start.12 = (pred[8,64]{1,0:T(8,128)(4,1)S(1)}, pred[8,64]{1,0:T(8,128)(4,1)}, u32[]{:S(2)}) copy-start(pred[8,64]{1,0:T(8,128)(4,1)} %add_compare_fusion) | copy-start | bytes 1540
  386.2 17.9 %copy-start.6 = (f32[4,64,64]{2,1,0:T(8,128)}, f32[4,64,64]{2,1,0:T(8,128)S(1)}, u32[]{:S(2)}) copy-start(f32[4,64,64]{2,1,0:T(8,128)S(1)} %get-tuple-element.47) | copy-start | bytes 196612
  386.2 8.4 %copy-start.15 = (f32[256]{0:T(256)S(1)}, f32[256]{0:T(256)}, u32[]{:S(2)}) copy-start(f32[256]{0:T(256)} %param.38) | copy-start | bytes 3076
  394.6 10.8 %copy-start.8 = (bf16[7,4096]{1,0:T(8,128)(2,1)S(1)}, bf16[7,4096]{1,0:T(8,128)(2,1)}, u32[]{:S(2)}) copy-start(bf16[7,4096]{1,0:T(8,128)(2,1)} %param.33) | copy-start | bytes 172036
  404.2 236.2 %all-gather.3.cloned.1.call-start = ((), (), s32[]{:S(2)}) async-start(), calls=%async_computation.5 | async-start | bytes 8257536 | tf_op jit(solution)/shard_map/all_gather | solution.py:175
  404.8 235.6 %all-gather.5.cloned.1.call-start = ((), (), s32[]{:S(2)}) async-start(), calls=%async_computation.6 | async-start | bytes 8257536 | tf_op jit(solution)/shard_map/all_gather | solution.py:176
  405.4 320.6 %reduce-scatter.2.cloned.1.call-start = ((), (), s32[]{:S(2)}) async-start(), calls=%async_computation.7 | async-start | bytes 4456448 | tf_op jit(solution)/shard_map/reduce_scatter | solution.py:182
  628.6 3.4 copy-start.3
  628.7 3.4 copy-start.10
  632.0 3.5 copy-start.2
  640.4 85.6 %copy-start.18 = (pred[512]{0:T(512)(128)(4,1)S(1)}, pred[512]{0:T(512)(128)(4,1)}, u32[]{:S(2)}) copy-start(pred[512]{0:T(512)(128)(4,1)} %copy-done.17) | copy-start | bytes 1540
Sparse Core Ops, SparseCore 0:
  404.3 219.1 all-reduce.1
  656.7 69.1 reduce-scatter.1
Sparse Core Ops, SparseCore 1:
  407.0 103.4 all-gather.2
  512.6 96.7 all-gather.4
